TPU v7x, 512 devices: a whole 4x4x16 slice. The times are simulated.
512 devices in a mesh: ctx: 32 (over z, core), tp: 16 (over x, y).
Axes of the slice: x: 4, y: 4, z: 16, core: 2. Of those that a mesh axis runs over, the one named last changes fastest.
Arguments:
- queries: bfloat16 [8192, 8192], P('ctx', 'tp'), may hold values from -6 to 6
- keys: bfloat16 [8192, 8192], P('ctx', 'tp'), may hold values from -0.0625 to 0.0625
- values: bfloat16 [8192, 8192], P('ctx', 'tp'), may hold values from -6 to 6
- log_keep: float32 [64, 8192], P('tp', 'ctx'), may hold values from -1 to 0, as said below
- state_in: float32 [64, 128, 128], P('tp'), may hold values from -6 to 6
- norm_gain: float32 [8192], P('tp'), may hold values from 0.1 to 1.9
- out_weight: bfloat16 [8192, 6144], P('tp', 'ctx'), may hold values from -0.125 to 0.125
Outputs:
- normed: bfloat16 [8192, 8192], P('ctx', 'tp')
- state_out: float32 [64, 128, 128], P('tp', 'ctx')
- layer_out: bfloat16 [8192, 6144], P('ctx', 'tp')
Inputs may be any that keep to these rules, and one draw needn't show every extreme that they name: `log_keep`: every entry is a logarithm of a keep factor, so at most 0.
All inputs are finite; a program needn't handle non-finite values.
Results may differ from a plain program's by a relative error of at most 0.014.
Values may be sent and summed in bfloat16 or wider, within the bound.
No kernel may reach another device: no remote copies, remote signals or barrier semaphores. Data moves between devices by JAX's collectives and lax.ppermute only.
A program may use at most 64 MiB of HBM per device.

v0:
```python
import jax
import jax.numpy as jnp
from jax import lax
from jax.sharding import PartitionSpec as P

H = 64
DH = 128
SPAN = 256
HIGH = lax.Precision.HIGHEST
EPSILON = 1e-06


def shifted(x, axis, by):
    peers = lax.axis_size(axis)
    pairs = [(i, i + by) for i in range(peers) if 0 <= i + by < peers]
    return lax.ppermute(x, axis, pairs)


def broadcast(x, axis, root):
    mine = lax.axis_index(axis) == root
    return lax.psum(jnp.where(mine, x, jnp.zeros_like(x)), axis)


def join_states(earlier, later):
    log_early, state_early = earlier
    log_late, state_late = later
    return (log_early + log_late, jnp.exp(log_late)[:, None, None] * state_early + state_late)


def close_chain(prev_log, prev_state, own_log, own_state, state_in):
    last_log, last_state = join_states((prev_log, prev_state), (own_log, own_state))
    return jnp.exp(last_log)[:, None, None] * state_in + last_state


def per_device(queries, keys, values, log_keep, state_in, norm_gain, out_weight):
    tokens_here = queries.shape[0]
    heads = log_keep.shape[0]
    width = state_in.shape[1]
    blocks = tokens_here // SPAN
    q_blocks = queries.reshape(blocks, SPAN, heads, width)
    k_blocks = keys.reshape(blocks, SPAN, heads, width)
    v_blocks = values.reshape(blocks, SPAN, heads, width)
    within = jnp.cumsum(log_keep.reshape(heads, blocks, SPAN), axis=2)
    causal = jnp.tril(jnp.ones((SPAN, SPAN), dtype=bool))
    spread = within[:, :, :, None] - within[:, :, None, :]
    decay = jnp.where(causal, jnp.exp(jnp.minimum(spread, 0.0)), 0.0)
    scores = jnp.einsum("cshd,cthd->hcst", q_blocks, k_blocks, preferred_element_type=jnp.float32)
    weights = (scores * decay).astype(jnp.bfloat16)
    intra = jnp.einsum("hcst,cthd->cshd", weights, v_blocks, preferred_element_type=jnp.float32)
    block_log = within[:, :, -1]
    key_factor = jnp.exp(block_log[:, :, None] - within).transpose(1, 2, 0)
    keys_decayed = (k_blocks * key_factor[:, :, :, None]).astype(jnp.bfloat16)
    increments = jnp.einsum(
        "cshd,cshe->chde", keys_decayed, v_blocks, preferred_element_type=jnp.float32
    )
    running = jnp.cumsum(block_log, axis=1)
    preceding_blocks = running - block_log
    order = jnp.arange(blocks)
    earlier_mask = order[None, :] < order[:, None]
    relative = preceding_blocks[:, :, None] - running[:, None, :]
    mixing = jnp.where(earlier_mask[None], jnp.exp(jnp.minimum(relative, 0.0)), 0.0)
    local_prefix = jnp.einsum("hcx,xhde->chde", mixing, increments, precision=HIGH)
    own_log = running[:, -1]
    own_state = jnp.einsum(
        "hc,chde->hde", jnp.exp(own_log[:, None] - running), increments, precision=HIGH
    )
    sequence_parts = lax.axis_size("ctx")
    zero_log = jnp.zeros_like(own_log)
    zero_state = jnp.zeros_like(own_state)

    def cycle_step(turn, carry):
        passed = join_states(carry, (own_log, own_state))
        return shifted((passed[0], passed[1]), "ctx", 1)

    prev_log, prev_state = lax.fori_loop(0, sequence_parts - 1, cycle_step, (zero_log, zero_state))
    closing = close_chain(prev_log, prev_state, own_log, own_state, state_in)
    shared_final = broadcast(closing, "ctx", sequence_parts - 1)
    share_rows = width // sequence_parts
    row_start = lax.axis_index("ctx") * share_rows
    final_share = lax.dynamic_slice_in_dim(shared_final, row_start, share_rows, 1)
    incoming_state = jnp.exp(prev_log)[:, None, None] * state_in + prev_state
    starts = jnp.exp(preceding_blocks).T[:, :, None, None] * incoming_state[None] + local_prefix
    starts_low = starts.astype(jnp.bfloat16)
    inter = jnp.einsum("cshd,chde->cshe", q_blocks, starts_low, preferred_element_type=jnp.float32)
    inter = inter * jnp.exp(within).transpose(1, 2, 0)[:, :, :, None]
    attended = (intra + inter).reshape(tokens_here, heads * width)
    squares = lax.psum(jnp.sum(attended * attended, axis=1), "tp")
    scale = lax.rsqrt(squares / (H * DH) + EPSILON)
    normed = (attended * scale[:, None] * norm_gain).astype(jnp.bfloat16)
    partials = jnp.dot(
        normed,
        lax.all_gather(out_weight, "ctx", axis=1, tiled=True),
        preferred_element_type=jnp.float32,
    )
    layer_out = lax.psum_scatter(
        partials.astype(jnp.bfloat16), "tp", scatter_dimension=1, tiled=True
    )
    return (normed, final_share, layer_out)


def solution(mesh):
    return jax.shard_map(
        per_device,
        mesh=mesh,
        in_specs=(
            P("ctx", "tp"),
            P("ctx", "tp"),
            P("ctx", "tp"),
            P("tp", "ctx"),
            P("tp", None, None),
            P("tp"),
            P("tp", "ctx"),
        ),
        out_specs=(P("ctx", "tp"), P("tp", "ctx", None), P("ctx", "tp")),
        check_vma=False,
    )
```

profile of v0, /device:TPU:2, one launch (start us, length us, event | category | flops | bytes accessed | tf_op | source)
XLA Modules:
  0.0 631.8 jit_solution(6297971191016926080)
XLA Ops:
  12.8 288.4 %while.13 = (s32[]{:T(128)}, f32[4]{0:T(128)S(1)}, f32[4,128,128]{2,1,0:T(8,128)S(1)}, f32[4]{0:T(128)S(1)}, f32[4,1,1]{0,2,1:T(1,128)S(1)}, /*index=5*/f32[4,128,128]{2,1,0:T(8,128)S(1)}, s32[]{:T(128)}) while((s32[]{:T(128)}, f32[4]{0:T(128)S(1)}, f32[4,128,128]{2,1,0:T(8,128)S(1)}, f32[4]{0:T(128)S(1)}, f32[4,1,1]{0,2,1:T(1,128)S(1)}, ...), condition=%wide.region_3.4_spmd, body=%wide.region_2.3_spmd.sunk | while | flops 131078 | bytes 1835293 | solution.py:75
  43.3 7.2 %collective-permute-start.1 = (f32[4,128,128]{2,1,0:T(8,128)S(1)}, f32[4,128,128]{2,1,0:T(8,128)S(1)}, u32[]{:S(2)}, u32[]{:S(2)}) collective-permute-start(f32[4,128,128]{2,1,0:T(8,128)S(1)} %multiply_add_fusion.2), channel_id=1, source_target_pairs={{0,16},{16,32},{32,48},{48,64},{64,80},{80,96},{96,112},{112,128},... | collective-permute-start | bytes 786440 | tf_op jit(solution)/shard_map/while/body/eval_jaxpr/ppermute | solution.py:16
  55.9 7.1 %collective-permute-start.1 = (f32[4,128,128]{2,1,0:T(8,128)S(1)}, f32[4,128,128]{2,1,0:T(8,128)S(1)}, u32[]{:S(2)}, u32[]{:S(2)}) collective-permute-start(f32[4,128,128]{2,1,0:T(8,128)S(1)} %multiply_add_fusion.2), channel_id=1, source_target_pairs={{0,16},{16,32},{32,48},{48,64},{64,80},{80,96},{96,112},{112,128},... | collective-permute-start | bytes 786440 | tf_op jit(solution)/shard_map/while/body/eval_jaxpr/ppermute | solution.py:16
  68.4 7.0 %collective-permute-start.1 = (f32[4,128,128]{2,1,0:T(8,128)S(1)}, f32[4,128,128]{2,1,0:T(8,128)S(1)}, u32[]{:S(2)}, u32[]{:S(2)}) collective-permute-start(f32[4,128,128]{2,1,0:T(8,128)S(1)} %multiply_add_fusion.2), channel_id=1, source_target_pairs={{0,16},{16,32},{32,48},{48,64},{64,80},{80,96},{96,112},{112,128},... | collective-permute-start | bytes 786440 | tf_op jit(solution)/shard_map/while/body/eval_jaxpr/ppermute | solution.py:16
  80.8 4.7 collective-permute-start.1
  93.7 4.5 collective-permute-start
  103.5 5.9 collective-permute-start
  112.9 5.6 collective-permute-start
  121.9 5.6 collective-permute-start
  131.0 5.6 collective-permute-start
  140.1 5.6 collective-permute-start
  149.2 5.6 collective-permute-start
  158.3 5.6 collective-permute-start
  167.4 5.6 collective-permute-start
  176.5 5.6 collective-permute-start
  185.6 5.6 collective-permute-start
  194.7 5.6 collective-permute-start
  203.8 5.6 collective-permute-start
  212.9 5.6 collective-permute-start
  221.9 5.6 collective-permute-start
  231.0 5.6 collective-permute-start
  240.1 5.6 collective-permute-start
  249.2 5.6 collective-permute-start
  258.3 5.6 collective-permute-start
  267.4 5.6 collective-permute-start
  276.5 5.6 collective-permute-start
  285.6 5.6 collective-permute-start
  294.7 5.6 collective-permute-start
  303.5 36.8 %psum.14 = f32[256]{0:T(256)S(1)} all-reduce(f32[256]{0:T(256)S(1)} %get-tuple-element.79), channel_id=1, replica_groups=mesh['ctx'=32,'tp'=16] {'tp'}, use_global_device_ids=true, to_apply=%region_5.6 | all-reduce | flops 256 | bytes 2048 | tf_op jit(solution)/shard_map/psum | solution.py:87
  341.1 4.7 convolution_convert_fusion
  348.6 178.8 %all-reduce.2.cloned.1.call-done = f32[4,128,128]{2,1,0:T(8,128)} async-done(((f32[4,128,128]{2,1,0:T(8,128)}), f32[4,128,128]{2,1,0:T(8,128)}) %all-reduce.2.cloned.1.call-update) | async-done | bytes 262160 | tf_op jit(solution)/shard_map/psum | solution.py:21
  528.7 94.8 %reduce-scatter.4.cloned.1.call-done = bf16[384,256]{1,0:T(8,128)(2,1)} async-done(((bf16[6144,256]{1,0:T(8,128)(2,1)}), bf16[384,256]{1,0:T(8,128)(2,1)}) %reduce-scatter.4.cloned.1.call-update) | async-done | bytes 196624
  (205 shorter events, 147.1 us)
Async XLA Ops:
  7.2 333.9 %all-gather.2.cloned.1.call-start = ((), (), s32[]{:S(2)}) async-start(), calls=%async_computation.2 | async-start | bytes 6488064 | tf_op jit(solution)/shard_map/all_gather | solution.py:92
  7.9 519.5 %all-reduce.2.cloned.1.call-start = ((), (), s32[]{:S(2)}) async-start(), calls=%async_computation.1 | async-start | bytes 524288 | tf_op jit(solution)/shard_map/psum | solution.py:21
  19.7 7.8 %collective-permute-start.1 = (f32[4,128,128]{2,1,0:T(8,128)S(1)}, f32[4,128,128]{2,1,0:T(8,128)S(1)}, u32[]{:S(2)}, u32[]{:S(2)}) collective-permute-start(f32[4,128,128]{2,1,0:T(8,128)S(1)} %multiply_add_fusion.2), channel_id=1, source_target_pairs={{0,16},{16,32},{32,48},{48,64},{64,80},{80,96},{96,112},{112,128},... | collective-permute-start | bytes 786440 | tf_op jit(solution)/shard_map/while/body/eval_jaxpr/ppermute | solution.py:16
  27.5 7.8 %collective-permute-start.1 = (f32[4,128,128]{2,1,0:T(8,128)S(1)}, f32[4,128,128]{2,1,0:T(8,128)S(1)}, u32[]{:S(2)}, u32[]{:S(2)}) collective-permute-start(f32[4,128,128]{2,1,0:T(8,128)S(1)} %multiply_add_fusion.2), channel_id=1, source_target_pairs={{0,16},{16,32},{32,48},{48,64},{64,80},{80,96},{96,112},{112,128},... | collective-permute-start | bytes 786440 | tf_op jit(solution)/shard_map/while/body/eval_jaxpr/ppermute | solution.py:16
  43.3 12.5 %collective-permute-start.1 = (f32[4,128,128]{2,1,0:T(8,128)S(1)}, f32[4,128,128]{2,1,0:T(8,128)S(1)}, u32[]{:S(2)}, u32[]{:S(2)}) collective-permute-start(f32[4,128,128]{2,1,0:T(8,128)S(1)} %multiply_add_fusion.2), channel_id=1, source_target_pairs={{0,16},{16,32},{32,48},{48,64},{64,80},{80,96},{96,112},{112,128},... | collective-permute-start | bytes 786440 | tf_op jit(solution)/shard_map/while/body/eval_jaxpr/ppermute | solution.py:16
  55.9 12.4 %collective-permute-start.1 = (f32[4,128,128]{2,1,0:T(8,128)S(1)}, f32[4,128,128]{2,1,0:T(8,128)S(1)}, u32[]{:S(2)}, u32[]{:S(2)}) collective-permute-start(f32[4,128,128]{2,1,0:T(8,128)S(1)} %multiply_add_fusion.2), channel_id=1, source_target_pairs={{0,16},{16,32},{32,48},{48,64},{64,80},{80,96},{96,112},{112,128},... | collective-permute-start | bytes 786440 | tf_op jit(solution)/shard_map/while/body/eval_jaxpr/ppermute | solution.py:16
  68.4 12.3 %collective-permute-start.1 = (f32[4,128,128]{2,1,0:T(8,128)S(1)}, f32[4,128,128]{2,1,0:T(8,128)S(1)}, u32[]{:S(2)}, u32[]{:S(2)}) collective-permute-start(f32[4,128,128]{2,1,0:T(8,128)S(1)} %multiply_add_fusion.2), channel_id=1, source_target_pairs={{0,16},{16,32},{32,48},{48,64},{64,80},{80,96},{96,112},{112,128},... | collective-permute-start | bytes 786440 | tf_op jit(solution)/shard_map/while/body/eval_jaxpr/ppermute | solution.py:16
  80.8 10.0 %collective-permute-start.1 = (f32[4,128,128]{2,1,0:T(8,128)S(1)}, f32[4,128,128]{2,1,0:T(8,128)S(1)}, u32[]{:S(2)}, u32[]{:S(2)}) collective-permute-start(f32[4,128,128]{2,1,0:T(8,128)S(1)} %multiply_add_fusion.2), channel_id=1, source_target_pairs={{0,16},{16,32},{32,48},{48,64},{64,80},{80,96},{96,112},{112,128},... | collective-permute-start | bytes 786440 | tf_op jit(solution)/shard_map/while/body/eval_jaxpr/ppermute | solution.py:16
  90.8 8.2 %collective-permute-start.1 = (f32[4,128,128]{2,1,0:T(8,128)S(1)}, f32[4,128,128]{2,1,0:T(8,128)S(1)}, u32[]{:S(2)}, u32[]{:S(2)}) collective-permute-start(f32[4,128,128]{2,1,0:T(8,128)S(1)} %multiply_add_fusion.2), channel_id=1, source_target_pairs={{0,16},{16,32},{32,48},{48,64},{64,80},{80,96},{96,112},{112,128},... | collective-permute-start | bytes 786440 | tf_op jit(solution)/shard_map/while/body/eval_jaxpr/ppermute | solution.py:16
  99.1 11.1 %collective-permute-start.1 = (f32[4,128,128]{2,1,0:T(8,128)S(1)}, f32[4,128,128]{2,1,0:T(8,128)S(1)}, u32[]{:S(2)}, u32[]{:S(2)}) collective-permute-start(f32[4,128,128]{2,1,0:T(8,128)S(1)} %multiply_add_fusion.2), channel_id=1, source_target_pairs={{0,16},{16,32},{32,48},{48,64},{64,80},{80,96},{96,112},{112,128},... | collective-permute-start | bytes 786440 | tf_op jit(solution)/shard_map/while/body/eval_jaxpr/ppermute | solution.py:16
  110.3 9.0 %collective-permute-start.1 = (f32[4,128,128]{2,1,0:T(8,128)S(1)}, f32[4,128,128]{2,1,0:T(8,128)S(1)}, u32[]{:S(2)}, u32[]{:S(2)}) collective-permute-start(f32[4,128,128]{2,1,0:T(8,128)S(1)} %multiply_add_fusion.2), channel_id=1, source_target_pairs={{0,16},{16,32},{32,48},{48,64},{64,80},{80,96},{96,112},{112,128},... | collective-permute-start | bytes 786440 | tf_op jit(solution)/shard_map/while/body/eval_jaxpr/ppermute | solution.py:16
  119.4 9.0 %collective-permute-start.1 = (f32[4,128,128]{2,1,0:T(8,128)S(1)}, f32[4,128,128]{2,1,0:T(8,128)S(1)}, u32[]{:S(2)}, u32[]{:S(2)}) collective-permute-start(f32[4,128,128]{2,1,0:T(8,128)S(1)} %multiply_add_fusion.2), channel_id=1, source_target_pairs={{0,16},{16,32},{32,48},{48,64},{64,80},{80,96},{96,112},{112,128},... | collective-permute-start | bytes 786440 | tf_op jit(solution)/shard_map/while/body/eval_jaxpr/ppermute | solution.py:16
  128.5 9.0 %collective-permute-start.1 = (f32[4,128,128]{2,1,0:T(8,128)S(1)}, f32[4,128,128]{2,1,0:T(8,128)S(1)}, u32[]{:S(2)}, u32[]{:S(2)}) collective-permute-start(f32[4,128,128]{2,1,0:T(8,128)S(1)} %multiply_add_fusion.2), channel_id=1, source_target_pairs={{0,16},{16,32},{32,48},{48,64},{64,80},{80,96},{96,112},{112,128},... | collective-permute-start | bytes 786440 | tf_op jit(solution)/shard_map/while/body/eval_jaxpr/ppermute | solution.py:16
  137.6 9.0 %collective-permute-start.1 = (f32[4,128,128]{2,1,0:T(8,128)S(1)}, f32[4,128,128]{2,1,0:T(8,128)S(1)}, u32[]{:S(2)}, u32[]{:S(2)}) collective-permute-start(f32[4,128,128]{2,1,0:T(8,128)S(1)} %multiply_add_fusion.2), channel_id=1, source_target_pairs={{0,16},{16,32},{32,48},{48,64},{64,80},{80,96},{96,112},{112,128},... | collective-permute-start | bytes 786440 | tf_op jit(solution)/shard_map/while/body/eval_jaxpr/ppermute | solution.py:16
  146.7 9.0 %collective-permute-start.1 = (f32[4,128,128]{2,1,0:T(8,128)S(1)}, f32[4,128,128]{2,1,0:T(8,128)S(1)}, u32[]{:S(2)}, u32[]{:S(2)}) collective-permute-start(f32[4,128,128]{2,1,0:T(8,128)S(1)} %multiply_add_fusion.2), channel_id=1, source_target_pairs={{0,16},{16,32},{32,48},{48,64},{64,80},{80,96},{96,112},{112,128},... | collective-permute-start | bytes 786440 | tf_op jit(solution)/shard_map/while/body/eval_jaxpr/ppermute | solution.py:16
  155.8 9.0 %collective-permute-start.1 = (f32[4,128,128]{2,1,0:T(8,128)S(1)}, f32[4,128,128]{2,1,0:T(8,128)S(1)}, u32[]{:S(2)}, u32[]{:S(2)}) collective-permute-start(f32[4,128,128]{2,1,0:T(8,128)S(1)} %multiply_add_fusion.2), channel_id=1, source_target_pairs={{0,16},{16,32},{32,48},{48,64},{64,80},{80,96},{96,112},{112,128},... | collective-permute-start | bytes 786440 | tf_op jit(solution)/shard_map/while/body/eval_jaxpr/ppermute | solution.py:16
  164.9 9.0 %collective-permute-start.1 = (f32[4,128,128]{2,1,0:T(8,128)S(1)}, f32[4,128,128]{2,1,0:T(8,128)S(1)}, u32[]{:S(2)}, u32[]{:S(2)}) collective-permute-start(f32[4,128,128]{2,1,0:T(8,128)S(1)} %multiply_add_fusion.2), channel_id=1, source_target_pairs={{0,16},{16,32},{32,48},{48,64},{64,80},{80,96},{96,112},{112,128},... | collective-permute-start | bytes 786440 | tf_op jit(solution)/shard_map/while/body/eval_jaxpr/ppermute | solution.py:16
  173.9 9.0 %collective-permute-start.1 = (f32[4,128,128]{2,1,0:T(8,128)S(1)}, f32[4,128,128]{2,1,0:T(8,128)S(1)}, u32[]{:S(2)}, u32[]{:S(2)}) collective-permute-start(f32[4,128,128]{2,1,0:T(8,128)S(1)} %multiply_add_fusion.2), channel_id=1, source_target_pairs={{0,16},{16,32},{32,48},{48,64},{64,80},{80,96},{96,112},{112,128},... | collective-permute-start | bytes 786440 | tf_op jit(solution)/shard_map/while/body/eval_jaxpr/ppermute | solution.py:16
  183.0 9.0 %collective-permute-start.1 = (f32[4,128,128]{2,1,0:T(8,128)S(1)}, f32[4,128,128]{2,1,0:T(8,128)S(1)}, u32[]{:S(2)}, u32[]{:S(2)}) collective-permute-start(f32[4,128,128]{2,1,0:T(8,128)S(1)} %multiply_add_fusion.2), channel_id=1, source_target_pairs={{0,16},{16,32},{32,48},{48,64},{64,80},{80,96},{96,112},{112,128},... | collective-permute-start | bytes 786440 | tf_op jit(solution)/shard_map/while/body/eval_jaxpr/ppermute | solution.py:16
  192.1 9.0 %collective-permute-start.1 = (f32[4,128,128]{2,1,0:T(8,128)S(1)}, f32[4,128,128]{2,1,0:T(8,128)S(1)}, u32[]{:S(2)}, u32[]{:S(2)}) collective-permute-start(f32[4,128,128]{2,1,0:T(8,128)S(1)} %multiply_add_fusion.2), channel_id=1, source_target_pairs={{0,16},{16,32},{32,48},{48,64},{64,80},{80,96},{96,112},{112,128},... | collective-permute-start | bytes 786440 | tf_op jit(solution)/shard_map/while/body/eval_jaxpr/ppermute | solution.py:16
  201.2 9.0 %collective-permute-start.1 = (f32[4,128,128]{2,1,0:T(8,128)S(1)}, f32[4,128,128]{2,1,0:T(8,128)S(1)}, u32[]{:S(2)}, u32[]{:S(2)}) collective-permute-start(f32[4,128,128]{2,1,0:T(8,128)S(1)} %multiply_add_fusion.2), channel_id=1, source_target_pairs={{0,16},{16,32},{32,48},{48,64},{64,80},{80,96},{96,112},{112,128},... | collective-permute-start | bytes 786440 | tf_op jit(solution)/shard_map/while/body/eval_jaxpr/ppermute | solution.py:16
  210.3 9.0 %collective-permute-start.1 = (f32[4,128,128]{2,1,0:T(8,128)S(1)}, f32[4,128,128]{2,1,0:T(8,128)S(1)}, u32[]{:S(2)}, u32[]{:S(2)}) collective-permute-start(f32[4,128,128]{2,1,0:T(8,128)S(1)} %multiply_add_fusion.2), channel_id=1, source_target_pairs={{0,16},{16,32},{32,48},{48,64},{64,80},{80,96},{96,112},{112,128},... | collective-permute-start | bytes 786440 | tf_op jit(solution)/shard_map/while/body/eval_jaxpr/ppermute | solution.py:16
  219.4 9.0 %collective-permute-start.1 = (f32[4,128,128]{2,1,0:T(8,128)S(1)}, f32[4,128,128]{2,1,0:T(8,128)S(1)}, u32[]{:S(2)}, u32[]{:S(2)}) collective-permute-start(f32[4,128,128]{2,1,0:T(8,128)S(1)} %multiply_add_fusion.2), channel_id=1, source_target_pairs={{0,16},{16,32},{32,48},{48,64},{64,80},{80,96},{96,112},{112,128},... | collective-permute-start | bytes 786440 | tf_op jit(solution)/shard_map/while/body/eval_jaxpr/ppermute | solution.py:16
  228.5 9.0 %collective-permute-start.1 = (f32[4,128,128]{2,1,0:T(8,128)S(1)}, f32[4,128,128]{2,1,0:T(8,128)S(1)}, u32[]{:S(2)}, u32[]{:S(2)}) collective-permute-start(f32[4,128,128]{2,1,0:T(8,128)S(1)} %multiply_add_fusion.2), channel_id=1, source_target_pairs={{0,16},{16,32},{32,48},{48,64},{64,80},{80,96},{96,112},{112,128},... | collective-permute-start | bytes 786440 | tf_op jit(solution)/shard_map/while/body/eval_jaxpr/ppermute | solution.py:16
  237.6 9.0 %collective-permute-start.1 = (f32[4,128,128]{2,1,0:T(8,128)S(1)}, f32[4,128,128]{2,1,0:T(8,128)S(1)}, u32[]{:S(2)}, u32[]{:S(2)}) collective-permute-start(f32[4,128,128]{2,1,0:T(8,128)S(1)} %multiply_add_fusion.2), channel_id=1, source_target_pairs={{0,16},{16,32},{32,48},{48,64},{64,80},{80,96},{96,112},{112,128},... | collective-permute-start | bytes 786440 | tf_op jit(solution)/shard_map/while/body/eval_jaxpr/ppermute | solution.py:16
  246.7 9.0 %collective-permute-start.1 = (f32[4,128,128]{2,1,0:T(8,128)S(1)}, f32[4,128,128]{2,1,0:T(8,128)S(1)}, u32[]{:S(2)}, u32[]{:S(2)}) collective-permute-start(f32[4,128,128]{2,1,0:T(8,128)S(1)} %multiply_add_fusion.2), channel_id=1, source_target_pairs={{0,16},{16,32},{32,48},{48,64},{64,80},{80,96},{96,112},{112,128},... | collective-permute-start | bytes 786440 | tf_op jit(solution)/shard_map/while/body/eval_jaxpr/ppermute | solution.py:16
  255.8 9.0 %collective-permute-start.1 = (f32[4,128,128]{2,1,0:T(8,128)S(1)}, f32[4,128,128]{2,1,0:T(8,128)S(1)}, u32[]{:S(2)}, u32[]{:S(2)}) collective-permute-start(f32[4,128,128]{2,1,0:T(8,128)S(1)} %multiply_add_fusion.2), channel_id=1, source_target_pairs={{0,16},{16,32},{32,48},{48,64},{64,80},{80,96},{96,112},{112,128},... | collective-permute-start | bytes 786440 | tf_op jit(solution)/shard_map/while/body/eval_jaxpr/ppermute | solution.py:16
  264.9 9.0 %collective-permute-start.1 = (f32[4,128,128]{2,1,0:T(8,128)S(1)}, f32[4,128,128]{2,1,0:T(8,128)S(1)}, u32[]{:S(2)}, u32[]{:S(2)}) collective-permute-start(f32[4,128,128]{2,1,0:T(8,128)S(1)} %multiply_add_fusion.2), channel_id=1, source_target_pairs={{0,16},{16,32},{32,48},{48,64},{64,80},{80,96},{96,112},{112,128},... | collective-permute-start | bytes 786440 | tf_op jit(solution)/shard_map/while/body/eval_jaxpr/ppermute | solution.py:16
  273.9 9.0 %collective-permute-start.1 = (f32[4,128,128]{2,1,0:T(8,128)S(1)}, f32[4,128,128]{2,1,0:T(8,128)S(1)}, u32[]{:S(2)}, u32[]{:S(2)}) collective-permute-start(f32[4,128,128]{2,1,0:T(8,128)S(1)} %multiply_add_fusion.2), channel_id=1, source_target_pairs={{0,16},{16,32},{32,48},{48,64},{64,80},{80,96},{96,112},{112,128},... | collective-permute-start | bytes 786440 | tf_op jit(solution)/shard_map/while/body/eval_jaxpr/ppermute | solution.py:16
  283.0 9.0 %collective-permute-start.1 = (f32[4,128,128]{2,1,0:T(8,128)S(1)}, f32[4,128,128]{2,1,0:T(8,128)S(1)}, u32[]{:S(2)}, u32[]{:S(2)}) collective-permute-start(f32[4,128,128]{2,1,0:T(8,128)S(1)} %multiply_add_fusion.2), channel_id=1, source_target_pairs={{0,16},{16,32},{32,48},{48,64},{64,80},{80,96},{96,112},{112,128},... | collective-permute-start | bytes 786440 | tf_op jit(solution)/shard_map/while/body/eval_jaxpr/ppermute | solution.py:16
  292.1 9.0 %collective-permute-start.1 = (f32[4,128,128]{2,1,0:T(8,128)S(1)}, f32[4,128,128]{2,1,0:T(8,128)S(1)}, u32[]{:S(2)}, u32[]{:S(2)}) collective-permute-start(f32[4,128,128]{2,1,0:T(8,128)S(1)} %multiply_add_fusion.2), channel_id=1, source_target_pairs={{0,16},{16,32},{32,48},{48,64},{64,80},{80,96},{96,112},{112,128},... | collective-permute-start | bytes 786440 | tf_op jit(solution)/shard_map/while/body/eval_jaxpr/ppermute | solution.py:16
  302.0 321.6 %reduce-scatter.4.cloned.1.call-start = ((), (), s32[]{:S(2)}) async-start(), calls=%async_computation.3 | async-start | bytes 3342336
  (37 other events, 1416.2 us)
Sparse Core Ops, SparseCore 0:
  10.1 82.4 all-gather.1
  302.1 225.2 all-reduce.1
  531.6 91.8 reduce-scatter.3
where the time goes:
time: 634 us; the launch traced here: 632 us
  waiting for transfers between devices  299 us (47%)
  starting transfers between devices  260 us (41%)
  blocking collectives  36.8 us (6%)
  between operations  13.9 us (2%)
  local copies, waits for them, and re-layouts  8.45 us (1%)
  matrix products  6.88 us (1%)
    ppermute x62, starting transfers between devices, shifted(): return lax.ppermute(x, axis, pairs)  260 us
    psum x1, waiting for transfers between devices, broadcast(): return lax.psum(jnp.where(mine, x, jnp.zeros_like(x)), axis)  179 us
    unnamed x4, waiting for transfers between devices  95.5 us
    psum x1, blocking collectives, per_device(): squares = lax.psum(jnp.sum(attended * attended, axis=1), 'tp')  36.8 us
    ppermute x62, waiting for transfers between devices, shifted(): return lax.ppermute(x, axis, pairs)  24.8 us
  transfers between devices with their start and end apart: 65, of which 33 were waited for; matrix products, arithmetic and copies ran while one was open for 3% of the time, Pallas kernels for 0%

commit v1 on v0

--- a/solution.py
+++ b/solution.py
@@ -2,6 +2,7 @@
 import jax.numpy as jnp
 from jax import lax
 from jax.sharding import PartitionSpec as P
+from jax.lax import all_gather
 
 H = 64
 DH = 128
@@ -18,7 +19,7 @@
 
 def broadcast(x, axis, root):
     mine = lax.axis_index(axis) == root
-    return lax.psum(jnp.where(mine, x, jnp.zeros_like(x)), axis)
+    return jnp.sum(all_gather(jnp.where(mine, x, jnp.zeros_like(x)), axis), 0)
 
 
 def join_states(earlier, later):

time: 634 us -> 499 us (0.79)
  waiting for transfers between devices: 299 us -> 161 us
    psum x1 -> x0, waiting for transfers between devices: 179 us -> none  [broadcast(): return lax.psum(jnp.where(mine, x, jnp.zeros_like(x)), axis)]
    all_gather x0 -> x1, waiting for transfers between devices: none -> 47.4 us  [broadcast(): return jnp.sum(all_gather(jnp.where(mine, x, jnp.zeros_like(x)), axis), 0)]
    unnamed x4, waiting for transfers between devices: 95.5 us -> 88.7 us
  transfers between devices with their start and end apart: 65 -> 65, of which waited for: 33 -> 33; matrix products, arithmetic and copies ran while one was open for 3% -> 5% of each run, Pallas kernels for 0% -> 0%
where the time goes in v1:
time: 499 us; the launch traced here: 497 us
  starting transfers between devices  260 us (52%)
  waiting for transfers between devices  161 us (32%)
  blocking collectives  36.8 us (7%)
  between operations  13.9 us (3%)
  other arithmetic  9.83 us (2%)
  local copies, waits for them, and re-layouts  7.77 us (2%)
  matrix products  6.92 us (1%)
    ppermute x62, starting transfers between devices, shifted(): return lax.ppermute(x, axis, pairs)  260 us
    unnamed x4, waiting for transfers between devices  88.7 us
    all_gather x1, waiting for transfers between devices, broadcast(): return jnp.sum(all_gather(jnp.where(mine, x, jnp.zeros_like(x)), axis), 0)  47.4 us
    psum x1, blocking collectives, per_device(): squares = lax.psum(jnp.sum(attended * attended, axis=1), 'tp')  36.8 us
    ppermute x62, waiting for transfers between devices, shifted(): return lax.ppermute(x, axis, pairs)  24.8 us
  transfers between devices with their start and end apart: 65, of which 33 were waited for; matrix products, arithmetic and copies ran while one was open for 5% of the time, Pallas kernels for 0%

profile of v1, /device:TPU:2, one launch (start us, length us, event | category | flops | bytes accessed | tf_op | source)
XLA Modules:
  0.0 496.8 jit_solution(9448950462982039869)
XLA Ops:
  12.8 288.4 %while.13 = (s32[]{:T(128)}, f32[4]{0:T(128)S(1)}, f32[4,128,128]{2,1,0:T(8,128)S(1)}, f32[4]{0:T(128)S(1)}, f32[4,1,1]{0,2,1:T(1,128)S(1)}, /*index=5*/f32[4,128,128]{2,1,0:T(8,128)S(1)}, s32[]{:T(128)}) while((s32[]{:T(128)}, f32[4]{0:T(128)S(1)}, f32[4,128,128]{2,1,0:T(8,128)S(1)}, f32[4]{0:T(128)S(1)}, f32[4,1,1]{0,2,1:T(1,128)S(1)}, ...), condition=%wide.region_3.4_spmd, body=%wide.region_2.3_spmd.sunk | while | flops 131078 | bytes 1835293 | solution.py:76
  43.3 7.2 %collective-permute-start.1 = (f32[4,128,128]{2,1,0:T(8,128)S(1)}, f32[4,128,128]{2,1,0:T(8,128)S(1)}, u32[]{:S(2)}, u32[]{:S(2)}) collective-permute-start(f32[4,128,128]{2,1,0:T(8,128)S(1)} %multiply_add_fusion.2), channel_id=1, source_target_pairs={{0,16},{16,32},{32,48},{48,64},{64,80},{80,96},{96,112},{112,128},... | collective-permute-start | bytes 786440 | tf_op jit(solution)/shard_map/while/body/eval_jaxpr/ppermute | solution.py:17
  55.9 7.1 %collective-permute-start.1 = (f32[4,128,128]{2,1,0:T(8,128)S(1)}, f32[4,128,128]{2,1,0:T(8,128)S(1)}, u32[]{:S(2)}, u32[]{:S(2)}) collective-permute-start(f32[4,128,128]{2,1,0:T(8,128)S(1)} %multiply_add_fusion.2), channel_id=1, source_target_pairs={{0,16},{16,32},{32,48},{48,64},{64,80},{80,96},{96,112},{112,128},... | collective-permute-start | bytes 786440 | tf_op jit(solution)/shard_map/while/body/eval_jaxpr/ppermute | solution.py:17
  68.4 7.0 %collective-permute-start.1 = (f32[4,128,128]{2,1,0:T(8,128)S(1)}, f32[4,128,128]{2,1,0:T(8,128)S(1)}, u32[]{:S(2)}, u32[]{:S(2)}) collective-permute-start(f32[4,128,128]{2,1,0:T(8,128)S(1)} %multiply_add_fusion.2), channel_id=1, source_target_pairs={{0,16},{16,32},{32,48},{48,64},{64,80},{80,96},{96,112},{112,128},... | collective-permute-start | bytes 786440 | tf_op jit(solution)/shard_map/while/body/eval_jaxpr/ppermute | solution.py:17
  80.8 4.7 collective-permute-start.1
  93.7 4.5 collective-permute-start
  103.5 5.9 %collective-permute-start = (f32[4]{0:T(128)S(1)}, f32[4]{0:T(128)S(1)}, u32[]{:S(2)}, u32[]{:S(2)}) collective-permute-start(f32[4]{0:T(128)S(1)} %add.74), channel_id=1, source_target_pairs={{0,16},{16,32},{32,48},{48,64},{64,80},{80,96},{96,112},{112,128},... | collective-permute-start | bytes 56 | tf_op jit(solution)/shard_map/while/body/eval_jaxpr/ppermute | solution.py:17
  112.9 5.6 %collective-permute-start = (f32[4]{0:T(128)S(1)}, f32[4]{0:T(128)S(1)}, u32[]{:S(2)}, u32[]{:S(2)}) collective-permute-start(f32[4]{0:T(128)S(1)} %add.74), channel_id=1, source_target_pairs={{0,16},{16,32},{32,48},{48,64},{64,80},{80,96},{96,112},{112,128},... | collective-permute-start | bytes 56 | tf_op jit(solution)/shard_map/while/body/eval_jaxpr/ppermute | solution.py:17
  121.9 5.6 %collective-permute-start = (f32[4]{0:T(128)S(1)}, f32[4]{0:T(128)S(1)}, u32[]{:S(2)}, u32[]{:S(2)}) collective-permute-start(f32[4]{0:T(128)S(1)} %add.74), channel_id=1, source_target_pairs={{0,16},{16,32},{32,48},{48,64},{64,80},{80,96},{96,112},{112,128},... | collective-permute-start | bytes 56 | tf_op jit(solution)/shard_map/while/body/eval_jaxpr/ppermute | solution.py:17
  131.0 5.6 %collective-permute-start = (f32[4]{0:T(128)S(1)}, f32[4]{0:T(128)S(1)}, u32[]{:S(2)}, u32[]{:S(2)}) collective-permute-start(f32[4]{0:T(128)S(1)} %add.74), channel_id=1, source_target_pairs={{0,16},{16,32},{32,48},{48,64},{64,80},{80,96},{96,112},{112,128},... | collective-permute-start | bytes 56 | tf_op jit(solution)/shard_map/while/body/eval_jaxpr/ppermute | solution.py:17
  140.1 5.6 %collective-permute-start = (f32[4]{0:T(128)S(1)}, f32[4]{0:T(128)S(1)}, u32[]{:S(2)}, u32[]{:S(2)}) collective-permute-start(f32[4]{0:T(128)S(1)} %add.74), channel_id=1, source_target_pairs={{0,16},{16,32},{32,48},{48,64},{64,80},{80,96},{96,112},{112,128},... | collective-permute-start | bytes 56 | tf_op jit(solution)/shard_map/while/body/eval_jaxpr/ppermute | solution.py:17
  149.2 5.6 %collective-permute-start = (f32[4]{0:T(128)S(1)}, f32[4]{0:T(128)S(1)}, u32[]{:S(2)}, u32[]{:S(2)}) collective-permute-start(f32[4]{0:T(128)S(1)} %add.74), channel_id=1, source_target_pairs={{0,16},{16,32},{32,48},{48,64},{64,80},{80,96},{96,112},{112,128},... | collective-permute-start | bytes 56 | tf_op jit(solution)/shard_map/while/body/eval_jaxpr/ppermute | solution.py:17
  158.3 5.6 %collective-permute-start = (f32[4]{0:T(128)S(1)}, f32[4]{0:T(128)S(1)}, u32[]{:S(2)}, u32[]{:S(2)}) collective-permute-start(f32[4]{0:T(128)S(1)} %add.74), channel_id=1, source_target_pairs={{0,16},{16,32},{32,48},{48,64},{64,80},{80,96},{96,112},{112,128},... | collective-permute-start | bytes 56 | tf_op jit(solution)/shard_map/while/body/eval_jaxpr/ppermute | solution.py:17
  167.4 5.6 %collective-permute-start = (f32[4]{0:T(128)S(1)}, f32[4]{0:T(128)S(1)}, u32[]{:S(2)}, u32[]{:S(2)}) collective-permute-start(f32[4]{0:T(128)S(1)} %add.74), channel_id=1, source_target_pairs={{0,16},{16,32},{32,48},{48,64},{64,80},{80,96},{96,112},{112,128},... | collective-permute-start | bytes 56 | tf_op jit(solution)/shard_map/while/body/eval_jaxpr/ppermute | solution.py:17
  176.5 5.6 %collective-permute-start = (f32[4]{0:T(128)S(1)}, f32[4]{0:T(128)S(1)}, u32[]{:S(2)}, u32[]{:S(2)}) collective-permute-start(f32[4]{0:T(128)S(1)} %add.74), channel_id=1, source_target_pairs={{0,16},{16,32},{32,48},{48,64},{64,80},{80,96},{96,112},{112,128},... | collective-permute-start | bytes 56 | tf_op jit(solution)/shard_map/while/body/eval_jaxpr/ppermute | solution.py:17
  185.6 5.6 %collective-permute-start = (f32[4]{0:T(128)S(1)}, f32[4]{0:T(128)S(1)}, u32[]{:S(2)}, u32[]{:S(2)}) collective-permute-start(f32[4]{0:T(128)S(1)} %add.74), channel_id=1, source_target_pairs={{0,16},{16,32},{32,48},{48,64},{64,80},{80,96},{96,112},{112,128},... | collective-permute-start | bytes 56 | tf_op jit(solution)/shard_map/while/body/eval_jaxpr/ppermute | solution.py:17
  194.7 5.6 %collective-permute-start = (f32[4]{0:T(128)S(1)}, f32[4]{0:T(128)S(1)}, u32[]{:S(2)}, u32[]{:S(2)}) collective-permute-start(f32[4]{0:T(128)S(1)} %add.74), channel_id=1, source_target_pairs={{0,16},{16,32},{32,48},{48,64},{64,80},{80,96},{96,112},{112,128},... | collective-permute-start | bytes 56 | tf_op jit(solution)/shard_map/while/body/eval_jaxpr/ppermute | solution.py:17
  203.8 5.6 %collective-permute-start = (f32[4]{0:T(128)S(1)}, f32[4]{0:T(128)S(1)}, u32[]{:S(2)}, u32[]{:S(2)}) collective-permute-start(f32[4]{0:T(128)S(1)} %add.74), channel_id=1, source_target_pairs={{0,16},{16,32},{32,48},{48,64},{64,80},{80,96},{96,112},{112,128},... | collective-permute-start | bytes 56 | tf_op jit(solution)/shard_map/while/body/eval_jaxpr/ppermute | solution.py:17
  212.9 5.6 %collective-permute-start = (f32[4]{0:T(128)S(1)}, f32[4]{0:T(128)S(1)}, u32[]{:S(2)}, u32[]{:S(2)}) collective-permute-start(f32[4]{0:T(128)S(1)} %add.74), channel_id=1, source_target_pairs={{0,16},{16,32},{32,48},{48,64},{64,80},{80,96},{96,112},{112,128},... | collective-permute-start | bytes 56 | tf_op jit(solution)/shard_map/while/body/eval_jaxpr/ppermute | solution.py:17
  221.9 5.6 %collective-permute-start = (f32[4]{0:T(128)S(1)}, f32[4]{0:T(128)S(1)}, u32[]{:S(2)}, u32[]{:S(2)}) collective-permute-start(f32[4]{0:T(128)S(1)} %add.74), channel_id=1, source_target_pairs={{0,16},{16,32},{32,48},{48,64},{64,80},{80,96},{96,112},{112,128},... | collective-permute-start | bytes 56 | tf_op jit(solution)/shard_map/while/body/eval_jaxpr/ppermute | solution.py:17
  231.0 5.6 %collective-permute-start = (f32[4]{0:T(128)S(1)}, f32[4]{0:T(128)S(1)}, u32[]{:S(2)}, u32[]{:S(2)}) collective-permute-start(f32[4]{0:T(128)S(1)} %add.74), channel_id=1, source_target_pairs={{0,16},{16,32},{32,48},{48,64},{64,80},{80,96},{96,112},{112,128},... | collective-permute-start | bytes 56 | tf_op jit(solution)/shard_map/while/body/eval_jaxpr/ppermute | solution.py:17
  240.1 5.6 %collective-permute-start = (f32[4]{0:T(128)S(1)}, f32[4]{0:T(128)S(1)}, u32[]{:S(2)}, u32[]{:S(2)}) collective-permute-start(f32[4]{0:T(128)S(1)} %add.74), channel_id=1, source_target_pairs={{0,16},{16,32},{32,48},{48,64},{64,80},{80,96},{96,112},{112,128},... | collective-permute-start | bytes 56 | tf_op jit(solution)/shard_map/while/body/eval_jaxpr/ppermute | solution.py:17
  249.2 5.6 %collective-permute-start = (f32[4]{0:T(128)S(1)}, f32[4]{0:T(128)S(1)}, u32[]{:S(2)}, u32[]{:S(2)}) collective-permute-start(f32[4]{0:T(128)S(1)} %add.74), channel_id=1, source_target_pairs={{0,16},{16,32},{32,48},{48,64},{64,80},{80,96},{96,112},{112,128},... | collective-permute-start | bytes 56 | tf_op jit(solution)/shard_map/while/body/eval_jaxpr/ppermute | solution.py:17
  258.3 5.6 %collective-permute-start = (f32[4]{0:T(128)S(1)}, f32[4]{0:T(128)S(1)}, u32[]{:S(2)}, u32[]{:S(2)}) collective-permute-start(f32[4]{0:T(128)S(1)} %add.74), channel_id=1, source_target_pairs={{0,16},{16,32},{32,48},{48,64},{64,80},{80,96},{96,112},{112,128},... | collective-permute-start | bytes 56 | tf_op jit(solution)/shard_map/while/body/eval_jaxpr/ppermute | solution.py:17
  267.4 5.6 %collective-permute-start = (f32[4]{0:T(128)S(1)}, f32[4]{0:T(128)S(1)}, u32[]{:S(2)}, u32[]{:S(2)}) collective-permute-start(f32[4]{0:T(128)S(1)} %add.74), channel_id=1, source_target_pairs={{0,16},{16,32},{32,48},{48,64},{64,80},{80,96},{96,112},{112,128},... | collective-permute-start | bytes 56 | tf_op jit(solution)/shard_map/while/body/eval_jaxpr/ppermute | solution.py:17
  276.5 5.6 %collective-permute-start = (f32[4]{0:T(128)S(1)}, f32[4]{0:T(128)S(1)}, u32[]{:S(2)}, u32[]{:S(2)}) collective-permute-start(f32[4]{0:T(128)S(1)} %add.74), channel_id=1, source_target_pairs={{0,16},{16,32},{32,48},{48,64},{64,80},{80,96},{96,112},{112,128},... | collective-permute-start | bytes 56 | tf_op jit(solution)/shard_map/while/body/eval_jaxpr/ppermute | solution.py:17
  285.6 5.6 %collective-permute-start = (f32[4]{0:T(128)S(1)}, f32[4]{0:T(128)S(1)}, u32[]{:S(2)}, u32[]{:S(2)}) collective-permute-start(f32[4]{0:T(128)S(1)} %add.74), channel_id=1, source_target_pairs={{0,16},{16,32},{32,48},{48,64},{64,80},{80,96},{96,112},{112,128},... | collective-permute-start | bytes 56 | tf_op jit(solution)/shard_map/while/body/eval_jaxpr/ppermute | solution.py:17
  294.7 5.6 %collective-permute-start = (f32[4]{0:T(128)S(1)}, f32[4]{0:T(128)S(1)}, u32[]{:S(2)}, u32[]{:S(2)}) collective-permute-start(f32[4]{0:T(128)S(1)} %add.74), channel_id=1, source_target_pairs={{0,16},{16,32},{32,48},{48,64},{64,80},{80,96},{96,112},{112,128},... | collective-permute-start | bytes 56 | tf_op jit(solution)/shard_map/while/body/eval_jaxpr/ppermute | solution.py:17
  303.5 36.8 %psum.7 = f32[256]{0:T(256)S(1)} all-reduce(f32[256]{0:T(256)S(1)} %get-tuple-element.79), channel_id=1, replica_groups=mesh['ctx'=32,'tp'=16] {'tp'}, use_global_device_ids=true, to_apply=%region_5.6 | all-reduce | flops 256 | bytes 2048 | tf_op jit(solution)/shard_map/psum | solution.py:88
  341.1 4.8 convolution_convert_fusion
  348.7 47.4 %all-gather.6.cloned.1.call-done = f32[128,128,128]{2,1,0:T(8,128)} async-done(((f32[4,128,128]{2,1,0:T(8,128)}), f32[128,128,128]{2,1,0:T(8,128)}) %all-gather.6.cloned.1.call-update) | async-done | bytes 8388624 | tf_op jit(solution)/shard_map/all_gather | solution.py:22
  400.6 88.0 %reduce-scatter.4.cloned.1.call-done = bf16[384,256]{1,0:T(8,128)(2,1)} async-done(((bf16[6144,256]{1,0:T(8,128)(2,1)}), bf16[384,256]{1,0:T(8,128)(2,1)}) %reduce-scatter.4.cloned.1.call-update) | async-done | bytes 196624
  (206 shorter events, 150.3 us)
Async XLA Ops:
  7.2 333.9 %all-gather.4.cloned.1.call-start = ((), (), s32[]{:S(2)}) async-start(), calls=%async_computation.1 | async-start | bytes 6488064 | tf_op jit(solution)/shard_map/all_gather | solution.py:93
  7.9 388.2 %all-gather.6.cloned.1.call-start = ((), (), s32[]{:S(2)}) async-start(), calls=%async_computation.2 | async-start | bytes 8650752 | tf_op jit(solution)/shard_map/all_gather | solution.py:22
  19.7 7.8 %collective-permute-start.1 = (f32[4,128,128]{2,1,0:T(8,128)S(1)}, f32[4,128,128]{2,1,0:T(8,128)S(1)}, u32[]{:S(2)}, u32[]{:S(2)}) collective-permute-start(f32[4,128,128]{2,1,0:T(8,128)S(1)} %multiply_add_fusion.2), channel_id=1, source_target_pairs={{0,16},{16,32},{32,48},{48,64},{64,80},{80,96},{96,112},{112,128},... | collective-permute-start | bytes 786440 | tf_op jit(solution)/shard_map/while/body/eval_jaxpr/ppermute | solution.py:17
  27.5 7.8 %collective-permute-start.1 = (f32[4,128,128]{2,1,0:T(8,128)S(1)}, f32[4,128,128]{2,1,0:T(8,128)S(1)}, u32[]{:S(2)}, u32[]{:S(2)}) collective-permute-start(f32[4,128,128]{2,1,0:T(8,128)S(1)} %multiply_add_fusion.2), channel_id=1, source_target_pairs={{0,16},{16,32},{32,48},{48,64},{64,80},{80,96},{96,112},{112,128},... | collective-permute-start | bytes 786440 | tf_op jit(solution)/shard_map/while/body/eval_jaxpr/ppermute | solution.py:17
  43.3 12.5 %collective-permute-start.1 = (f32[4,128,128]{2,1,0:T(8,128)S(1)}, f32[4,128,128]{2,1,0:T(8,128)S(1)}, u32[]{:S(2)}, u32[]{:S(2)}) collective-permute-start(f32[4,128,128]{2,1,0:T(8,128)S(1)} %multiply_add_fusion.2), channel_id=1, source_target_pairs={{0,16},{16,32},{32,48},{48,64},{64,80},{80,96},{96,112},{112,128},... | collective-permute-start | bytes 786440 | tf_op jit(solution)/shard_map/while/body/eval_jaxpr/ppermute | solution.py:17
  55.9 12.4 %collective-permute-start.1 = (f32[4,128,128]{2,1,0:T(8,128)S(1)}, f32[4,128,128]{2,1,0:T(8,128)S(1)}, u32[]{:S(2)}, u32[]{:S(2)}) collective-permute-start(f32[4,128,128]{2,1,0:T(8,128)S(1)} %multiply_add_fusion.2), channel_id=1, source_target_pairs={{0,16},{16,32},{32,48},{48,64},{64,80},{80,96},{96,112},{112,128},... | collective-permute-start | bytes 786440 | tf_op jit(solution)/shard_map/while/body/eval_jaxpr/ppermute | solution.py:17
  68.4 12.3 %collective-permute-start.1 = (f32[4,128,128]{2,1,0:T(8,128)S(1)}, f32[4,128,128]{2,1,0:T(8,128)S(1)}, u32[]{:S(2)}, u32[]{:S(2)}) collective-permute-start(f32[4,128,128]{2,1,0:T(8,128)S(1)} %multiply_add_fusion.2), channel_id=1, source_target_pairs={{0,16},{16,32},{32,48},{48,64},{64,80},{80,96},{96,112},{112,128},... | collective-permute-start | bytes 786440 | tf_op jit(solution)/shard_map/while/body/eval_jaxpr/ppermute | solution.py:17
  80.8 10.0 %collective-permute-start.1 = (f32[4,128,128]{2,1,0:T(8,128)S(1)}, f32[4,128,128]{2,1,0:T(8,128)S(1)}, u32[]{:S(2)}, u32[]{:S(2)}) collective-permute-start(f32[4,128,128]{2,1,0:T(8,128)S(1)} %multiply_add_fusion.2), channel_id=1, source_target_pairs={{0,16},{16,32},{32,48},{48,64},{64,80},{80,96},{96,112},{112,128},... | collective-permute-start | bytes 786440 | tf_op jit(solution)/shard_map/while/body/eval_jaxpr/ppermute | solution.py:17
  90.8 8.2 %collective-permute-start.1 = (f32[4,128,128]{2,1,0:T(8,128)S(1)}, f32[4,128,128]{2,1,0:T(8,128)S(1)}, u32[]{:S(2)}, u32[]{:S(2)}) collective-permute-start(f32[4,128,128]{2,1,0:T(8,128)S(1)} %multiply_add_fusion.2), channel_id=1, source_target_pairs={{0,16},{16,32},{32,48},{48,64},{64,80},{80,96},{96,112},{112,128},... | collective-permute-start | bytes 786440 | tf_op jit(solution)/shard_map/while/body/eval_jaxpr/ppermute | solution.py:17
  99.1 11.1 %collective-permute-start.1 = (f32[4,128,128]{2,1,0:T(8,128)S(1)}, f32[4,128,128]{2,1,0:T(8,128)S(1)}, u32[]{:S(2)}, u32[]{:S(2)}) collective-permute-start(f32[4,128,128]{2,1,0:T(8,128)S(1)} %multiply_add_fusion.2), channel_id=1, source_target_pairs={{0,16},{16,32},{32,48},{48,64},{64,80},{80,96},{96,112},{112,128},... | collective-permute-start | bytes 786440 | tf_op jit(solution)/shard_map/while/body/eval_jaxpr/ppermute | solution.py:17
  110.3 9.0 %collective-permute-start.1 = (f32[4,128,128]{2,1,0:T(8,128)S(1)}, f32[4,128,128]{2,1,0:T(8,128)S(1)}, u32[]{:S(2)}, u32[]{:S(2)}) collective-permute-start(f32[4,128,128]{2,1,0:T(8,128)S(1)} %multiply_add_fusion.2), channel_id=1, source_target_pairs={{0,16},{16,32},{32,48},{48,64},{64,80},{80,96},{96,112},{112,128},... | collective-permute-start | bytes 786440 | tf_op jit(solution)/shard_map/while/body/eval_jaxpr/ppermute | solution.py:17
  119.4 9.0 %collective-permute-start.1 = (f32[4,128,128]{2,1,0:T(8,128)S(1)}, f32[4,128,128]{2,1,0:T(8,128)S(1)}, u32[]{:S(2)}, u32[]{:S(2)}) collective-permute-start(f32[4,128,128]{2,1,0:T(8,128)S(1)} %multiply_add_fusion.2), channel_id=1, source_target_pairs={{0,16},{16,32},{32,48},{48,64},{64,80},{80,96},{96,112},{112,128},... | collective-permute-start | bytes 786440 | tf_op jit(solution)/shard_map/while/body/eval_jaxpr/ppermute | solution.py:17
  128.5 9.0 %collective-permute-start.1 = (f32[4,128,128]{2,1,0:T(8,128)S(1)}, f32[4,128,128]{2,1,0:T(8,128)S(1)}, u32[]{:S(2)}, u32[]{:S(2)}) collective-permute-start(f32[4,128,128]{2,1,0:T(8,128)S(1)} %multiply_add_fusion.2), channel_id=1, source_target_pairs={{0,16},{16,32},{32,48},{48,64},{64,80},{80,96},{96,112},{112,128},... | collective-permute-start | bytes 786440 | tf_op jit(solution)/shard_map/while/body/eval_jaxpr/ppermute | solution.py:17
  137.6 9.0 %collective-permute-start.1 = (f32[4,128,128]{2,1,0:T(8,128)S(1)}, f32[4,128,128]{2,1,0:T(8,128)S(1)}, u32[]{:S(2)}, u32[]{:S(2)}) collective-permute-start(f32[4,128,128]{2,1,0:T(8,128)S(1)} %multiply_add_fusion.2), channel_id=1, source_target_pairs={{0,16},{16,32},{32,48},{48,64},{64,80},{80,96},{96,112},{112,128},... | collective-permute-start | bytes 786440 | tf_op jit(solution)/shard_map/while/body/eval_jaxpr/ppermute | solution.py:17
  146.7 9.0 %collective-permute-start.1 = (f32[4,128,128]{2,1,0:T(8,128)S(1)}, f32[4,128,128]{2,1,0:T(8,128)S(1)}, u32[]{:S(2)}, u32[]{:S(2)}) collective-permute-start(f32[4,128,128]{2,1,0:T(8,128)S(1)} %multiply_add_fusion.2), channel_id=1, source_target_pairs={{0,16},{16,32},{32,48},{48,64},{64,80},{80,96},{96,112},{112,128},... | collective-permute-start | bytes 786440 | tf_op jit(solution)/shard_map/while/body/eval_jaxpr/ppermute | solution.py:17
  155.8 9.0 %collective-permute-start.1 = (f32[4,128,128]{2,1,0:T(8,128)S(1)}, f32[4,128,128]{2,1,0:T(8,128)S(1)}, u32[]{:S(2)}, u32[]{:S(2)}) collective-permute-start(f32[4,128,128]{2,1,0:T(8,128)S(1)} %multiply_add_fusion.2), channel_id=1, source_target_pairs={{0,16},{16,32},{32,48},{48,64},{64,80},{80,96},{96,112},{112,128},... | collective-permute-start | bytes 786440 | tf_op jit(solution)/shard_map/while/body/eval_jaxpr/ppermute | solution.py:17
  164.9 9.0 %collective-permute-start.1 = (f32[4,128,128]{2,1,0:T(8,128)S(1)}, f32[4,128,128]{2,1,0:T(8,128)S(1)}, u32[]{:S(2)}, u32[]{:S(2)}) collective-permute-start(f32[4,128,128]{2,1,0:T(8,128)S(1)} %multiply_add_fusion.2), channel_id=1, source_target_pairs={{0,16},{16,32},{32,48},{48,64},{64,80},{80,96},{96,112},{112,128},... | collective-permute-start | bytes 786440 | tf_op jit(solution)/shard_map/while/body/eval_jaxpr/ppermute | solution.py:17
  173.9 9.0 %collective-permute-start.1 = (f32[4,128,128]{2,1,0:T(8,128)S(1)}, f32[4,128,128]{2,1,0:T(8,128)S(1)}, u32[]{:S(2)}, u32[]{:S(2)}) collective-permute-start(f32[4,128,128]{2,1,0:T(8,128)S(1)} %multiply_add_fusion.2), channel_id=1, source_target_pairs={{0,16},{16,32},{32,48},{48,64},{64,80},{80,96},{96,112},{112,128},... | collective-permute-start | bytes 786440 | tf_op jit(solution)/shard_map/while/body/eval_jaxpr/ppermute | solution.py:17
  183.0 9.0 %collective-permute-start.1 = (f32[4,128,128]{2,1,0:T(8,128)S(1)}, f32[4,128,128]{2,1,0:T(8,128)S(1)}, u32[]{:S(2)}, u32[]{:S(2)}) collective-permute-start(f32[4,128,128]{2,1,0:T(8,128)S(1)} %multiply_add_fusion.2), channel_id=1, source_target_pairs={{0,16},{16,32},{32,48},{48,64},{64,80},{80,96},{96,112},{112,128},... | collective-permute-start | bytes 786440 | tf_op jit(solution)/shard_map/while/body/eval_jaxpr/ppermute | solution.py:17
  192.1 9.0 %collective-permute-start.1 = (f32[4,128,128]{2,1,0:T(8,128)S(1)}, f32[4,128,128]{2,1,0:T(8,128)S(1)}, u32[]{:S(2)}, u32[]{:S(2)}) collective-permute-start(f32[4,128,128]{2,1,0:T(8,128)S(1)} %multiply_add_fusion.2), channel_id=1, source_target_pairs={{0,16},{16,32},{32,48},{48,64},{64,80},{80,96},{96,112},{112,128},... | collective-permute-start | bytes 786440 | tf_op jit(solution)/shard_map/while/body/eval_jaxpr/ppermute | solution.py:17
  201.2 9.0 %collective-permute-start.1 = (f32[4,128,128]{2,1,0:T(8,128)S(1)}, f32[4,128,128]{2,1,0:T(8,128)S(1)}, u32[]{:S(2)}, u32[]{:S(2)}) collective-permute-start(f32[4,128,128]{2,1,0:T(8,128)S(1)} %multiply_add_fusion.2), channel_id=1, source_target_pairs={{0,16},{16,32},{32,48},{48,64},{64,80},{80,96},{96,112},{112,128},... | collective-permute-start | bytes 786440 | tf_op jit(solution)/shard_map/while/body/eval_jaxpr/ppermute | solution.py:17
  210.3 9.0 %collective-permute-start.1 = (f32[4,128,128]{2,1,0:T(8,128)S(1)}, f32[4,128,128]{2,1,0:T(8,128)S(1)}, u32[]{:S(2)}, u32[]{:S(2)}) collective-permute-start(f32[4,128,128]{2,1,0:T(8,128)S(1)} %multiply_add_fusion.2), channel_id=1, source_target_pairs={{0,16},{16,32},{32,48},{48,64},{64,80},{80,96},{96,112},{112,128},... | collective-permute-start | bytes 786440 | tf_op jit(solution)/shard_map/while/body/eval_jaxpr/ppermute | solution.py:17
  219.4 9.0 %collective-permute-start.1 = (f32[4,128,128]{2,1,0:T(8,128)S(1)}, f32[4,128,128]{2,1,0:T(8,128)S(1)}, u32[]{:S(2)}, u32[]{:S(2)}) collective-permute-start(f32[4,128,128]{2,1,0:T(8,128)S(1)} %multiply_add_fusion.2), channel_id=1, source_target_pairs={{0,16},{16,32},{32,48},{48,64},{64,80},{80,96},{96,112},{112,128},... | collective-permute-start | bytes 786440 | tf_op jit(solution)/shard_map/while/body/eval_jaxpr/ppermute | solution.py:17
  228.5 9.0 %collective-permute-start.1 = (f32[4,128,128]{2,1,0:T(8,128)S(1)}, f32[4,128,128]{2,1,0:T(8,128)S(1)}, u32[]{:S(2)}, u32[]{:S(2)}) collective-permute-start(f32[4,128,128]{2,1,0:T(8,128)S(1)} %multiply_add_fusion.2), channel_id=1, source_target_pairs={{0,16},{16,32},{32,48},{48,64},{64,80},{80,96},{96,112},{112,128},... | collective-permute-start | bytes 786440 | tf_op jit(solution)/shard_map/while/body/eval_jaxpr/ppermute | solution.py:17
  237.6 9.0 %collective-permute-start.1 = (f32[4,128,128]{2,1,0:T(8,128)S(1)}, f32[4,128,128]{2,1,0:T(8,128)S(1)}, u32[]{:S(2)}, u32[]{:S(2)}) collective-permute-start(f32[4,128,128]{2,1,0:T(8,128)S(1)} %multiply_add_fusion.2), channel_id=1, source_target_pairs={{0,16},{16,32},{32,48},{48,64},{64,80},{80,96},{96,112},{112,128},... | collective-permute-start | bytes 786440 | tf_op jit(solution)/shard_map/while/body/eval_jaxpr/ppermute | solution.py:17
  246.7 9.0 %collective-permute-start.1 = (f32[4,128,128]{2,1,0:T(8,128)S(1)}, f32[4,128,128]{2,1,0:T(8,128)S(1)}, u32[]{:S(2)}, u32[]{:S(2)}) collective-permute-start(f32[4,128,128]{2,1,0:T(8,128)S(1)} %multiply_add_fusion.2), channel_id=1, source_target_pairs={{0,16},{16,32},{32,48},{48,64},{64,80},{80,96},{96,112},{112,128},... | collective-permute-start | bytes 786440 | tf_op jit(solution)/shard_map/while/body/eval_jaxpr/ppermute | solution.py:17
  255.8 9.0 %collective-permute-start.1 = (f32[4,128,128]{2,1,0:T(8,128)S(1)}, f32[4,128,128]{2,1,0:T(8,128)S(1)}, u32[]{:S(2)}, u32[]{:S(2)}) collective-permute-start(f32[4,128,128]{2,1,0:T(8,128)S(1)} %multiply_add_fusion.2), channel_id=1, source_target_pairs={{0,16},{16,32},{32,48},{48,64},{64,80},{80,96},{96,112},{112,128},... | collective-permute-start | bytes 786440 | tf_op jit(solution)/shard_map/while/body/eval_jaxpr/ppermute | solution.py:17
  264.9 9.0 %collective-permute-start.1 = (f32[4,128,128]{2,1,0:T(8,128)S(1)}, f32[4,128,128]{2,1,0:T(8,128)S(1)}, u32[]{:S(2)}, u32[]{:S(2)}) collective-permute-start(f32[4,128,128]{2,1,0:T(8,128)S(1)} %multiply_add_fusion.2), channel_id=1, source_target_pairs={{0,16},{16,32},{32,48},{48,64},{64,80},{80,96},{96,112},{112,128},... | collective-permute-start | bytes 786440 | tf_op jit(solution)/shard_map/while/body/eval_jaxpr/ppermute | solution.py:17
  273.9 9.0 %collective-permute-start.1 = (f32[4,128,128]{2,1,0:T(8,128)S(1)}, f32[4,128,128]{2,1,0:T(8,128)S(1)}, u32[]{:S(2)}, u32[]{:S(2)}) collective-permute-start(f32[4,128,128]{2,1,0:T(8,128)S(1)} %multiply_add_fusion.2), channel_id=1, source_target_pairs={{0,16},{16,32},{32,48},{48,64},{64,80},{80,96},{96,112},{112,128},... | collective-permute-start | bytes 786440 | tf_op jit(solution)/shard_map/while/body/eval_jaxpr/ppermute | solution.py:17
  283.0 9.0 %collective-permute-start.1 = (f32[4,128,128]{2,1,0:T(8,128)S(1)}, f32[4,128,128]{2,1,0:T(8,128)S(1)}, u32[]{:S(2)}, u32[]{:S(2)}) collective-permute-start(f32[4,128,128]{2,1,0:T(8,128)S(1)} %multiply_add_fusion.2), channel_id=1, source_target_pairs={{0,16},{16,32},{32,48},{48,64},{64,80},{80,96},{96,112},{112,128},... | collective-permute-start | bytes 786440 | tf_op jit(solution)/shard_map/while/body/eval_jaxpr/ppermute | solution.py:17
  292.1 9.0 %collective-permute-start.1 = (f32[4,128,128]{2,1,0:T(8,128)S(1)}, f32[4,128,128]{2,1,0:T(8,128)S(1)}, u32[]{:S(2)}, u32[]{:S(2)}) collective-permute-start(f32[4,128,128]{2,1,0:T(8,128)S(1)} %multiply_add_fusion.2), channel_id=1, source_target_pairs={{0,16},{16,32},{32,48},{48,64},{64,80},{80,96},{96,112},{112,128},... | collective-permute-start | bytes 786440 | tf_op jit(solution)/shard_map/while/body/eval_jaxpr/ppermute | solution.py:17
  302.0 186.5 %reduce-scatter.4.cloned.1.call-start = ((), (), s32[]{:S(2)}) async-start(), calls=%async_computation.3 | async-start | bytes 3342336
  (37 other events, 1416.3 us)
Sparse Core Ops, SparseCore 0:
  10.1 82.4 all-gather.3
  302.1 93.9 all-gather.5
  400.3 88.1 reduce-scatter.3
